TPU v7x, 256 devices: a whole 4x4x8 slice. The times are simulated.
256 devices in a mesh: inst: 16 (over x, y), page: 8 (over z), head: 2 (over core).
Axes of the slice: x: 4, y: 4, z: 8, core: 2. Of those that a mesh axis runs over, the one named last changes fastest.
Arguments:
- queries: bfloat16 [32, 8192], P('inst', 'head'), may hold values from -21 to 21
- fresh_key_value: bfloat16 [2, 32, 1024], P(None, 'inst', 'head'), may hold values from -8 to 8
- key_value_pool: bfloat16 [2, 16384, 16, 1024], P(None, ('inst', 'page'), None, 'head'), may hold values from -21 to 21
- block_table: int32 [32, 768], P('inst'), may hold values from -1 to 16383, as said below
- lengths: int32 [32], P('inst'), may hold values from 17 to 12288, as said below
Outputs:
- attn: bfloat16 [32, 8192], P('inst', 'head')
Inputs may be any that keep to these rules, and one draw needn't show every extreme that they name: `block_table`: request r is owned by instance r // 2. Entries 0 to ceil(lengths[r] / 16) - 1 of row r are pool page numbers below 16384, distinct over all requests; every other entry is -1. `lengths`: every request has two or more pages; some request has exactly 768 full pages.
All inputs are finite; a program needn't handle non-finite values.
Results may differ from a plain program's by a relative error of at most 0.001.
Values may be sent and summed in bfloat16 or wider, within the bound.
No kernel may reach another device: no remote copies, remote signals or barrier semaphores. Data moves between devices by JAX's collectives and lax.ppermute only.
A program may use at most 192 MiB of HBM per device.

v0:
```python
import math
import jax
import jax.numpy as jnp
from jax import lax
from jax.sharding import PartitionSpec as P

HEAD_SIZE = 128
LOWEST_SCORE = -1e30


def slot_owners(all_tables, all_lengths, slots, page_tok):
    requests, most_pages = all_tables.shape
    first_page = (lax.axis_index("inst") * lax.axis_size("page") + lax.axis_index("page")) * slots
    column = jnp.arange(most_pages, dtype=jnp.int32)
    live_page = column[None, :] * page_tok < all_lengths[:, None]
    local_page = all_tables - first_page
    inside = live_page & (local_page >= 0) & (local_page < slots)
    expected_output = jnp.where(inside, local_page, slots).reshape(-1)
    request_ids = jnp.broadcast_to(
        jnp.arange(requests, dtype=jnp.int32)[:, None], (requests, most_pages)
    ).reshape(-1)
    page_fill = jnp.clip(all_lengths[:, None] - column[None, :] * page_tok, 0, page_tok).reshape(-1)
    page_owner = (
        jnp.full((slots,), requests, jnp.int32).at[expected_output].set(request_ids, mode="drop")
    )
    filled = jnp.zeros((slots,), jnp.int32).at[expected_output].set(page_fill, mode="drop")
    return (page_owner, filled)


def page_partials(slot_queries, key_value_pool, filled):
    slots = key_value_pool.shape[1]
    page_tok = key_value_pool.shape[2]
    groups = key_value_pool.shape[3] // HEAD_SIZE
    heads = slot_queries.shape[1] // HEAD_SIZE
    grouped_queries = slot_queries.reshape(slots, groups, heads // groups, HEAD_SIZE)
    paged_keys = key_value_pool[0].reshape(slots, page_tok, groups, HEAD_SIZE)
    paged_values = key_value_pool[1].reshape(slots, page_tok, groups, HEAD_SIZE)
    scores = jnp.einsum(
        "sgqd,stgd->sgqt", grouped_queries, paged_keys, preferred_element_type=jnp.float32
    ) * (1.0 / math.sqrt(HEAD_SIZE))
    offsets = jnp.arange(page_tok, dtype=jnp.int32)
    valid = (offsets[None, :] < filled[:, None])[:, None, None, :]
    masked = jnp.where(valid, scores, LOWEST_SCORE)
    page_max = jnp.max(masked, axis=3)
    raw_weight = jnp.where(valid, jnp.exp(masked - page_max[..., None]), 0.0)
    page_sum = jnp.sum(raw_weight, axis=3)
    page_out = jnp.einsum(
        "sgqt,stgd->sgqd",
        raw_weight.astype(jnp.bfloat16),
        paged_values,
        preferred_element_type=jnp.float32,
    )
    return (
        page_max.reshape(slots, heads),
        page_sum.reshape(slots, heads),
        page_out.reshape(slots, heads * HEAD_SIZE),
    )


def request_max(page_max, page_owner, requests):
    matches = page_owner[None, :] == jnp.arange(requests, dtype=jnp.int32)[:, None]
    return jnp.max(jnp.where(matches[:, :, None], page_max[None], LOWEST_SCORE), axis=1)


def request_sums(page_max, page_sum, page_out, page_owner, shared_max):
    requests, heads = shared_max.shape
    slots = page_max.shape[0]
    padded = jnp.concatenate([shared_max, jnp.full((1, heads), LOWEST_SCORE, jnp.float32)], axis=0)
    factor = jnp.exp(page_max - padded[page_owner])
    one_hot = (page_owner[None, :] == jnp.arange(requests, dtype=jnp.int32)[:, None]).astype(
        jnp.float32
    )
    scaled_out = (page_out.reshape(slots, heads, HEAD_SIZE) * factor[:, :, None]).reshape(
        slots, heads * HEAD_SIZE
    )
    summed_out = jnp.dot(
        one_hot, scaled_out, precision=lax.Precision.HIGHEST, preferred_element_type=jnp.float32
    )
    summed_total = jnp.dot(
        one_hot,
        page_sum * factor,
        precision=lax.Precision.HIGHEST,
        preferred_element_type=jnp.float32,
    )
    return (summed_total, summed_out)


def finish(queries, fresh_key_value, cache_max, cache_total, cache_out):
    own_rows = queries.shape[0]
    heads = queries.shape[1] // HEAD_SIZE
    groups = fresh_key_value.shape[2] // HEAD_SIZE
    per_group = heads // groups
    grouped_queries = queries.reshape(own_rows, groups, per_group, HEAD_SIZE)
    new_keys = fresh_key_value[0].reshape(own_rows, groups, HEAD_SIZE)
    fresh_score = jnp.einsum(
        "rgqd,rgd->rgq", grouped_queries, new_keys, preferred_element_type=jnp.float32
    ).reshape(own_rows, heads) * (1.0 / math.sqrt(HEAD_SIZE))
    top_score = jnp.maximum(cache_max, fresh_score)
    carried = jnp.exp(cache_max - top_score)
    own_weight = jnp.exp(fresh_score - top_score)
    denominator = own_weight + cache_total * carried
    new_values = jnp.broadcast_to(
        fresh_key_value[1].astype(jnp.float32).reshape(own_rows, groups, 1, HEAD_SIZE),
        (own_rows, groups, per_group, HEAD_SIZE),
    ).reshape(own_rows, heads, HEAD_SIZE)
    weighted = (
        own_weight[:, :, None] * new_values
        + cache_out.reshape(own_rows, heads, HEAD_SIZE) * carried[:, :, None]
    )
    return (
        (weighted / denominator[:, :, None])
        .reshape(own_rows, heads * HEAD_SIZE)
        .astype(jnp.bfloat16)
    )


def shards(queries, fresh_key_value, key_value_pool, block_table, lengths):
    all_tables, all_lengths = (
        lax.all_gather(block_table, "inst", axis=0, tiled=True),
        lax.all_gather(lengths, "inst", axis=0, tiled=True),
    )
    all_queries = lax.all_gather(queries, "inst", axis=0, tiled=True)
    requests = all_tables.shape[0]
    own_rows = queries.shape[0]
    row_start = lax.axis_index("inst") * own_rows
    page_owner, filled = slot_owners(
        all_tables, all_lengths, key_value_pool.shape[1], key_value_pool.shape[2]
    )
    slot_queries = all_queries[jnp.minimum(page_owner, requests - 1)]
    page_max, page_sum, page_out = page_partials(slot_queries, key_value_pool, filled)
    local_max = request_max(page_max, page_owner, requests)
    shared_max = lax.pmax(local_max, ("inst", "page"))
    shared_total, shared_out = request_sums(page_max, page_sum, page_out, page_owner, shared_max)
    summed_out, summed_total = lax.psum((shared_out, shared_total), ("inst", "page"))
    cache_max = lax.dynamic_slice_in_dim(shared_max, row_start, own_rows, 0)
    cache_total = lax.dynamic_slice_in_dim(summed_total, row_start, own_rows, 0)
    cache_out = lax.dynamic_slice_in_dim(summed_out, row_start, own_rows, 0)
    return finish(queries, fresh_key_value, cache_max, cache_total, cache_out)


def solution(mesh):
    return jax.shard_map(
        shards,
        mesh=mesh,
        in_specs=(
            P("inst", "head"),
            P(None, "inst", "head"),
            P(None, ("inst", "page"), None, "head"),
            P("inst", None),
            P("inst"),
        ),
        out_specs=P("inst", "head"),
        check_vma=False,
    )
```

profile of v0, /device:TPU:0, one launch (start us, length us, event | category | flops | bytes accessed | tf_op | source)
XLA Modules:
  0.0 1664.2 jit_solution(2714726597789726109)
XLA Ops:
  6.5 1.3 dynamic-slice
  8.5 0.9 dynamic-update-slice
  9.3 14.7 all-reduce.1
  24.0 21.6 %all-gather = s32[16,2,768]{2,1,0:T(2,128)S(1)} all-gather(s32[1,2,768]{2,1,0:T(2,128)} %bitcast.89), channel_id=1, replica_groups=mesh['inst'=16,'page'=8,'head'=2] {'inst'}, dimensions={0}, use_global_device_ids=true | all-gather | bytes 104448 | tf_op jit(solution)/shard_map/all_gather | solution.py:119
  46.1 90.2 %scatter_custom_fusion = s32[128]{0:T(128)S(1)} fusion(s32[24576]{0:T(1024)S(1)} %bitcast.84, s32[24576]{0:T(1024)S(1)} %reshape.155, s32[]{:T(128)} %constant.17.clone.1), kind=kCustom, calls=%fused_computation.59 | custom fusion | bytes 516 | tf_op jit(solution)/shard_map/scatter | solution.py:24
  136.3 90.2 %scatter_custom_fusion.1 = s32[128]{0:T(128)S(1)} fusion(s32[24576]{0:T(1024)S(1)} %bitcast.85, s32[24576]{0:T(1024)S(1)} %reshape.163, s32[]{:T(128)} %constant.5.clone.1), kind=kCustom, calls=%fused_computation.57 | custom fusion | bytes 516 | tf_op jit(solution)/shard_map/scatter | solution.py:26
  226.6 22.9 %all-gather.1 = bf16[16,2,4096]{2,1,0:T(2,128)(2,1)S(1)} all-gather(bf16[1,2,4096]{2,1,0:T(2,128)(2,1)} %bitcast.87), channel_id=1, replica_groups=mesh['inst'=16,'page'=8,'head'=2] {'inst'}, dimensions={0}, use_global_device_ids=true | all-gather | bytes 278528 | tf_op jit(solution)/shard_map/all_gather | solution.py:122
  249.6 1.2 gather_fusion
  250.8 0.2 copy.37
  251.0 4.6 fusion.34
  255.6 3.5 copy.34
  259.1 3.0 copy.27
  262.1 3.5 copy.33
  265.6 3.0 copy.24
  268.5 2.9 fusion.4
  271.9 689.7 %pmax.7 = f32[32,32]{1,0:T(8,128)S(1)} all-reduce(f32[32,32]{1,0:T(8,128)S(1)} %select_reduce_fusion), channel_id=1, replica_groups=mesh['inst'=16,'page'=8,'head'=2] {'inst','page'}, use_global_device_ids=true, to_apply=%region_4.5 | all-reduce | flops 1024 | bytes 8192 | tf_op jit(solution)/shard_map/pmax | solution.py:132
  961.6 3.7 fusion.7
  965.3 0.6 gather_fusion.1
  966.0 0.6 mul.86
  966.6 1.0 copy-done
  967.6 4.3 fusion
  971.9 1.4 fusion.5
  973.9 681.6 %psum.15 = f32[32,32]{1,0:T(8,128)S(1)} all-reduce(f32[32,32]{1,0:T(8,128)S(1)} %fusion.14), channel_id=1, replica_groups=mesh['inst'=16,'page'=8,'head'=2] {'inst','page'}, use_global_device_ids=true, to_apply=%region_7.8 | all-reduce | flops 1024 | bytes 8192 | tf_op jit(solution)/shard_map/psum | solution.py:134
  1655.7 1.6 fusion.17
  (42 shorter events, 1.9 us)
Async XLA Ops:
  6.5 1649.2 %all-reduce.4.cloned.1.call-start = ((), (), s32[]{:S(2)}) async-start(), calls=%async_computation | async-start | bytes 1048576 | tf_op jit(solution)/shard_map/psum | solution.py:134
  966.0 1.6 copy-start
  971.9 1.4 copy-start.2
  971.9 1.4 copy-start.1
Sparse Core Ops, SparseCore 0:
  972.0 207.2 all-reduce.3
where the time goes:
time: 1660 us
  blocking collectives  1430 us (86%)
  local copies, waits for them, and re-layouts  205 us (12%)
    pmax x1, blocking collectives, shards(): shared_max = lax.pmax(local_max, ('inst', 'page'))  690 us
    psum x1, blocking collectives, shards(): lax.psum((shared_out, shared_total), ('inst', 'page'))  682 us
    scatter x1, local copies, waits for them, and re-layouts, slot_owners(): jnp.full((slots,), requests, jnp.int32).at[expected_output]  90.2 us
    scatter x1, local copies, waits for them, and re-layouts, slot_owners(): jnp.zeros((slots,), jnp.int32).at[expected_output]  90.2 us
  transfers between devices with their start and end apart: 1, of which 0 were waited for; matrix products, arithmetic and copies ran while one was open for 0% of the time, Pallas kernels for 0%

commit v1 on v0

--- a/solution.py
+++ b/solution.py
@@ -131,7 +131,7 @@
     local_max = request_max(page_max, page_owner, requests)
     shared_max = lax.pmax(local_max, ("inst", "page"))
     shared_total, shared_out = request_sums(page_max, page_sum, page_out, page_owner, shared_max)
-    summed_out, summed_total = lax.psum((shared_out, shared_total), ("inst", "page"))
+    summed_out, summed_total = lax.psum(lax.psum((shared_out, shared_total), "inst"), "page")
     cache_max = lax.dynamic_slice_in_dim(shared_max, row_start, own_rows, 0)
     cache_total = lax.dynamic_slice_in_dim(summed_total, row_start, own_rows, 0)
     cache_out = lax.dynamic_slice_in_dim(summed_out, row_start, own_rows, 0)

time: 1660 us -> 1150 us (0.69)
  blocking collectives: 1430 us -> 845 us
  waiting for transfers between devices: 0.04 us -> 65.7 us
    psum x1 -> x2, blocking collectives: 682 us -> 96.6 us  [the longest x1 69.5 us: shards(): lax.psum((shared_out, shared_total), 'inst')]
    psum x1 -> x2, waiting for transfers between devices: 0.02 us -> 65.6 us  [the longest x1 65.6 us: shards(): lax.psum(lax.psum((shared_out, shared_total), 'inst'), 'page')]
  transfers between devices with their start and end apart: 1 -> 2, of which waited for: 0 -> 1; matrix products, arithmetic and copies ran while one was open for 0% -> 0% of each run, Pallas kernels for 0% -> 0%
where the time goes in v1:
time: 1150 us; the launch traced here: 1140 us
  blocking collectives  845 us (73%)
  local copies, waits for them, and re-layouts  205 us (18%)
  waiting for transfers between devices  65.7 us (6%)
  between operations  14.3 us (1%)
    pmax x1, blocking collectives, shards(): shared_max = lax.pmax(local_max, ('inst', 'page'))  690 us
    scatter x1, local copies, waits for them, and re-layouts, slot_owners(): jnp.full((slots,), requests, jnp.int32).at[expected_output]  90.2 us
    scatter x1, local copies, waits for them, and re-layouts, slot_owners(): jnp.zeros((slots,), jnp.int32).at[expected_output]  90.2 us
    psum x1, blocking collectives, shards(): lax.psum((shared_out, shared_total), 'inst')  69.5 us
    psum x1, waiting for transfers between devices, shards(): lax.psum(lax.psum((shared_out, shared_total), 'inst'), 'page')  65.6 us
    psum x1, blocking collectives, shards(): lax.psum(lax.psum((shared_out, shared_total), 'inst'), 'page')  27.1 us
  transfers between devices with their start and end apart: 2, of which 1 were waited for; matrix products, arithmetic and copies ran while one was open for 0% of the time, Pallas kernels for 0%

profile of v1, /device:TPU:0, one launch (start us, length us, event | category | flops | bytes accessed | tf_op | source)
XLA Modules:
  0.0 1144.9 jit_solution(15967436512820563978)
XLA Ops:
  6.5 1.3 dynamic-slice
  8.5 0.9 dynamic-update-slice
  9.3 14.7 %all-reduce.1 = s32[32]{0:T(128)S(1)} all-reduce(s32[32]{0:T(128)S(1)} %dynamic-update-slice), channel_id=1, replica_groups=mesh['inst'=16,'page'=8,'head'=2] {'inst'}, use_global_device_ids=true, to_apply=%add.1 | all-reduce | flops 32 | bytes 256
  24.0 21.6 %all-gather = s32[16,2,768]{2,1,0:T(2,128)S(1)} all-gather(s32[1,2,768]{2,1,0:T(2,128)} %bitcast.89), channel_id=1, replica_groups=mesh['inst'=16,'page'=8,'head'=2] {'inst'}, dimensions={0}, use_global_device_ids=true | all-gather | bytes 104448 | tf_op jit(solution)/shard_map/all_gather | solution.py:119
  46.1 90.2 %scatter_custom_fusion = s32[128]{0:T(128)S(1)} fusion(s32[24576]{0:T(1024)S(1)} %bitcast.84, s32[24576]{0:T(1024)S(1)} %reshape.155, s32[]{:T(128)} %constant.17.clone.1), kind=kCustom, calls=%fused_computation.59 | custom fusion | bytes 516 | tf_op jit(solution)/shard_map/scatter | solution.py:24
  136.3 90.2 %scatter_custom_fusion.1 = s32[128]{0:T(128)S(1)} fusion(s32[24576]{0:T(1024)S(1)} %bitcast.85, s32[24576]{0:T(1024)S(1)} %reshape.163, s32[]{:T(128)} %constant.5.clone.1), kind=kCustom, calls=%fused_computation.57 | custom fusion | bytes 516 | tf_op jit(solution)/shard_map/scatter | solution.py:26
  226.6 22.9 %all-gather.1 = bf16[16,2,4096]{2,1,0:T(2,128)(2,1)S(1)} all-gather(bf16[1,2,4096]{2,1,0:T(2,128)(2,1)} %bitcast.87), channel_id=1, replica_groups=mesh['inst'=16,'page'=8,'head'=2] {'inst'}, dimensions={0}, use_global_device_ids=true | all-gather | bytes 278528 | tf_op jit(solution)/shard_map/all_gather | solution.py:122
  249.6 1.2 gather_fusion
  251.0 4.6 fusion.34
  255.6 3.5 copy.34
  259.1 3.0 copy.27
  262.1 3.5 copy.33
  265.6 3.0 copy.24
  268.5 2.9 fusion.4
  271.9 689.7 %pmax.7 = f32[32,32]{1,0:T(8,128)S(1)} all-reduce(f32[32,32]{1,0:T(8,128)S(1)} %select_reduce_fusion), channel_id=1, replica_groups=mesh['inst'=16,'page'=8,'head'=2] {'inst','page'}, use_global_device_ids=true, to_apply=%region_4.5 | all-reduce | flops 1024 | bytes 8192 | tf_op jit(solution)/shard_map/pmax | solution.py:132
  961.6 3.7 fusion.7
  965.3 0.6 gather_fusion.1
  966.6 1.0 copy-done
  967.6 4.3 fusion
  972.0 1.4 fusion.5
  974.0 69.5 %psum.30 = f32[32,32]{1,0:T(8,128)S(1)} all-reduce(f32[32,32]{1,0:T(8,128)S(1)} %fusion.14), channel_id=1, replica_groups=mesh['inst'=16,'page'=8,'head'=2] {'inst'}, use_global_device_ids=true, to_apply=%region_8.9 | all-reduce | flops 1024 | bytes 8192 | tf_op jit(solution)/shard_map/psum | solution.py:134
  1043.5 27.1 %psum.31 = f32[32,32]{1,0:T(8,128)S(1)} all-reduce(f32[32,32]{1,0:T(8,128)S(1)} %psum.30), channel_id=1, replica_groups=mesh['inst'=16,'page'=8,'head'=2] {'page'}, use_global_device_ids=true, to_apply=%region_9.10 | all-reduce | flops 1024 | bytes 8192 | tf_op jit(solution)/shard_map/psum | solution.py:134
  1070.8 65.6 %all-reduce.7.cloned.1.call-done = f32[32,4096]{1,0:T(8,128)} async-done(((f32[32,4096]{1,0:T(8,128)}), f32[32,4096]{1,0:T(8,128)}) %all-reduce.7.cloned.1.call-update) | async-done | bytes 524304 | tf_op jit(solution)/shard_map/psum | solution.py:134
  1136.4 1.6 fusion.17
  (46 shorter events, 2.8 us)
Async XLA Ops:
  6.5 1064.1 %all-reduce.5.cloned.1.call-start = ((), (), s32[]{:S(2)}) async-start(), calls=%async_computation | async-start | bytes 1048576 | tf_op jit(solution)/shard_map/psum | solution.py:134
  966.0 1.6 copy-start
  971.9 1.5 copy-start.2
  971.9 1.5 copy-start.1
  971.9 164.5 %all-reduce.7.cloned.1.call-start = ((), (), s32[]{:S(2)}) async-start(), calls=%async_computation.1 | async-start | bytes 1048576 | tf_op jit(solution)/shard_map/psum | solution.py:134
Sparse Core Ops, SparseCore 0:
  972.0 86.1 all-reduce.4
  1070.8 65.5 all-reduce.6
